TPU v7x, 32 devices: a whole 2x2x4 slice. The times are simulated.
32 devices in a mesh: run: 1, row: 16 (over z, y, core), col: 1, seg: 2 (over x).
Axes of the slice: x: 2, y: 2, z: 4, core: 2. Of those that a mesh axis runs over, the one named last changes fastest.
Arguments:
- traces: bfloat16 [2, 1024, 2048], P(('run', 'seg'), 'row', 'col'), may hold values from -30 to 30
- live_mask: int32 [1024], P(('run', 'row')), may hold values 0 or 1
- sources: int32 [64], replicated, may hold values from 0 to 1023
- owners: int32 [64, 1], replicated, may hold values from 0 to 15; in each aligned block of 64 rows (0 to 63, 64 to 127, ...) at most 12 rows name the same one
Outputs:
- gathers: bfloat16 [192, 16, 64, 256], P(('run', 'row'), None, ('col', 'seg'))
Inputs may be any that keep to these rules, and one draw needn't show every extreme that they name: `owners`: at most 12 sources share an owner, and some owner has exactly 12.
All inputs are finite; a program needn't handle non-finite values. No bound on the sum of `live_mask` on one device may be relied on, other than what follows from the above.
Results may differ from a plain program's by a relative error of at most 0.024.
Values may be sent and summed in bfloat16 or wider, within the bound.
No kernel may reach another device: no remote copies, remote signals or barrier semaphores. Data moves between devices by JAX's collectives and lax.ppermute only.
A program may use at most 64 MiB of HBM per device.

v0:
```python
import math
import jax
import jax.numpy as jnp
from jax import lax
from jax.sharding import PartitionSpec as P

NT = 2048
NF = 1024
LAGS = 256
BAND = 64
two_pi = 2.0 * math.pi


def turn_table(first_ids, second_ids, period):
    product = first_ids[:, None] * second_ids[None, :] % period
    return product.astype(jnp.float32) * (two_pi / period)


def lag_matrix(bin_ids):
    lag_ids = jnp.arange(LAGS, dtype=jnp.int32) - LAGS // 2 + NT
    lag_angles = turn_table(bin_ids, lag_ids, NT)
    return jnp.concatenate(
        [jnp.cos(lag_angles).astype(jnp.bfloat16), -jnp.sin(lag_angles).astype(jnp.bfloat16)],
        axis=0,
    )


def correlate(recv_real, recv_imag, real_source, imag_source, lag_table):
    cross_real = (
        real_source[:, None, :] * recv_real[:, :, None]
        + imag_source[:, None, :] * recv_imag[:, :, None]
    ).astype(jnp.bfloat16)
    cross_imag = (
        imag_source[:, None, :] * recv_real[:, :, None]
        - real_source[:, None, :] * recv_imag[:, :, None]
    ).astype(jnp.bfloat16)
    stacked_cross = jnp.concatenate([cross_real, cross_imag], axis=0)
    return jnp.einsum("fl,fgv->gvl", lag_table, stacked_cross, preferred_element_type=jnp.float32)


def local(traces, live_mask, sources, owners):
    col_count = lax.axis_size("col")
    seg_count = lax.axis_size("seg")
    row_count = lax.axis_size("row")
    samples = traces[0]
    channels = samples.shape[0]
    local_width = samples.shape[1]
    num_sources = sources.shape[0]
    first_sample = lax.axis_index("col") * local_width
    half_bins = NF // col_count
    sample_ids = first_sample + jnp.arange(local_width, dtype=jnp.int32)
    bin_ids = jnp.arange(half_bins * lax.axis_size("col"), dtype=jnp.int32)
    angles = turn_table(sample_ids, bin_ids, NT)
    cosine = jnp.cos(angles).astype(jnp.bfloat16)
    sine_table = jnp.sin(angles).astype(jnp.bfloat16)
    real_part = jnp.einsum("tf,ct->fc", cosine, samples, preferred_element_type=jnp.float32)
    imag_part = -jnp.einsum("tf,ct->fc", sine_table, samples, preferred_element_type=jnp.float32)
    spectra = lax.psum_scatter(
        jnp.concatenate([real_part, imag_part], axis=1).astype(jnp.bfloat16),
        "col",
        scatter_dimension=0,
        tiled=True,
    ).astype(jnp.float32)
    squares = (spectra * spectra).reshape(half_bins // BAND, BAND, 2, channels)
    band_power = jnp.sum(squares, axis=(1, 2)) / (2 * BAND) + 1e-05
    scaling = live_mask.astype(jnp.float32)[None, :] / jnp.sqrt(band_power)
    scaling = jnp.repeat(scaling, BAND, axis=0)
    whitened = (
        (spectra.reshape(half_bins, 2, channels) * scaling[:, None, :])
        .reshape(half_bins, 2 * channels)
        .astype(jnp.bfloat16)
    )
    white_real = whitened[:, :channels]
    white_imag = whitened[:, channels:]
    everyone = lax.all_gather(whitened, "row", axis=1, tiled=True)
    block_ids = sources // channels
    within = sources % channels
    real_cols = block_ids * (2 * channels) + within
    source_real = jnp.take(everyone, real_cols, axis=1)
    source_imag = jnp.take(everyone, real_cols + channels, axis=1)
    receivers = channels // (col_count * seg_count)
    bin_ids = lax.axis_index("col") * half_bins + jnp.arange(half_bins, dtype=jnp.int32)
    lag_table = lag_matrix(bin_ids)
    real_source = source_real.astype(jnp.float32)
    imag_source = source_imag.astype(jnp.float32)

    def one_group(offset):
        recv_real = lax.dynamic_slice_in_dim(white_real, offset, receivers, 1).astype(jnp.float32)
        recv_imag = lax.dynamic_slice_in_dim(white_imag, offset, receivers, 1).astype(jnp.float32)
        return correlate(recv_real, recv_imag, real_source, imag_source, lag_table)

    offsets = (
        jnp.arange(receivers * lax.axis_size(("col", "seg")) // receivers, dtype=jnp.int32)
        * receivers
    )
    blocks = lax.map(one_group, offsets)
    stacked = lax.psum_scatter(
        blocks.reshape(receivers * lax.axis_size(("col", "seg")), num_sources, LAGS).astype(
            jnp.bfloat16
        ),
        ("col", "seg"),
        scatter_dimension=0,
        tiled=True,
    ).astype(jnp.float32)
    mean_sq = jnp.mean(stacked * stacked, axis=-1, keepdims=True)
    normed = (stacked / jnp.sqrt(mean_sq + 1e-06)).astype(jnp.bfloat16)
    capacity = 3 * num_sources // row_count
    owner_ids = owners[:, 0]
    order_ids = jnp.arange(num_sources, dtype=jnp.int32)
    earlier = (owner_ids[:, None] == owner_ids[None, :]) & (order_ids[None, :] < order_ids[:, None])
    slot_rank = jnp.sum(earlier.astype(jnp.int32), axis=1)
    slot_ids = owner_ids * capacity + slot_rank
    placing = (
        jnp.arange(row_count * capacity, dtype=jnp.int32)[:, None] == slot_ids[None, :]
    ).astype(jnp.bfloat16)
    outgoing = jnp.einsum(
        "sv,gvl->sgl", placing, normed, preferred_element_type=jnp.float32
    ).astype(jnp.bfloat16)
    return lax.all_to_all(outgoing[:, None], "row", split_axis=0, concat_axis=1, tiled=True)


def solution(mesh):
    placed = (P(("run", "seg"), "row", "col"), P(("run", "row")), P(), P())
    return jax.shard_map(
        local,
        mesh=mesh,
        in_specs=placed,
        out_specs=P(("run", "row"), None, ("col", "seg"), None),
        check_vma=False,
    )
```

profile of v0, /device:TPU:1, one launch (start us, length us, event | category | flops | bytes accessed | tf_op | source)
XLA Modules:
  0.0 271.0 jit_solution(1408020758581116476)
XLA Ops:
  6.5 0.0 copy-start
  6.5 0.0 all-gather.2.cloned.1.call-start
  6.5 0.9 copy-done
  7.5 31.3 %fusion.21 = bf16[1024,64]{0,1:T(8,128)(2,1)S(1)} fusion(bf16[1,64,2048]{2,1,0:T(8,128)(2,1)S(1)} %copy-done), kind=kOutput, calls=%fused_computation.35 | convolution fusion | flops 300023808 | bytes 393216 | tf_op jit(solution)/shard_map/tf,ct->fc/dot_general | solution.py:57
  38.8 0.0 copy-start.4
  38.8 31.2 %fusion.22 = bf16[1024,64]{0,1:T(8,128)(2,1)S(1)} fusion(bf16[1,64,2048]{2,1,0:T(8,128)(2,1)S(1)} %copy-done), kind=kOutput, calls=%fused_computation.36 | convolution fusion | flops 299958272 | bytes 393216 | tf_op jit(solution)/shard_map/tf,ct->fc/dot_general | solution.py:56
  70.1 0.0 copy-start.3
  70.1 0.3 mul.149
  70.4 0.2 reduce_sum.28
  70.6 0.1 copy.15
  70.7 0.0 copy-done.4
  70.7 0.1 copy.16
  70.8 0.2 broadcast_in_dim.19
  71.0 0.2 mul.150
  71.2 0.8 multiply_convert_fusion
  72.0 0.0 all-gather.2.cloned.1.call-update
  72.0 0.0 reduce-scatter.2.cloned.1.call-start
  72.1 0.0 copy-done.3
  72.1 1.0 fusion.48
  73.1 4.2 %cosine_convert_fusion.4 = bf16[1024,256]{1,0:T(8,128)(2,1)S(1)} fusion(s32[256]{0:T(256)S(1)} %iota_add_fusion), kind=kLoop, calls=%fused_computation.43 | loop fusion | flops 3932160 | bytes 525312 | tf_op jit(solution)/shard_map/convert_element_type | solution.py:23
  77.3 4.0 %fusion.31 = bf16[1024,256]{1,0:T(8,128)(2,1)S(1)} fusion(s32[256]{0:T(256)S(1)} %iota_add_fusion), kind=kLoop, calls=%fused_computation.47 | loop fusion | flops 4718592 | bytes 525312 | tf_op jit(solution)/shard_map/neg | solution.py:23
  81.4 1.0 pad_maximum_fusion
  82.4 42.7 %all-gather.2.cloned.1.call-done = bf16[1024,2048]{0,1:T(8,128)(2,1)} async-done(((bf16[1024,128]{0,1:T(8,128)(2,1)}), bf16[1024,2048]{0,1:T(8,128)(2,1)}) %all-gather.2.cloned.1.call-update) | async-done | bytes 4194320 | tf_op jit(solution)/shard_map/all_gather | solution.py:75
  125.1 3.5 %gather_fusion = bf16[64,1024]{1,0:T(8,128)(2,1)S(1)} fusion(bf16[1024,2048]{0,1:T(8,128)(2,1)} %all-gather.2.cloned.1.call-done, s32[1024]{0:T(1024)S(1)} %pad_clamp_fusion.1), kind=kCustom, calls=%fused_computation.clone | custom fusion | bytes 262400 | tf_op jit(solution)/shard_map/jit(_take)/gather | solution.py:79
  128.6 3.5 %gather_fusion.1 = bf16[64,1024]{1,0:T(8,128)(2,1)S(1)} fusion(bf16[1024,2048]{0,1:T(8,128)(2,1)} %all-gather.2.cloned.1.call-done, s32[1024]{0:T(1024)S(1)} %pad_clamp_fusion), kind=kCustom, calls=%fused_computation.1.clone | custom fusion | bytes 262400 | tf_op jit(solution)/shard_map/jit(_take)/gather | solution.py:80
  132.2 0.1 bitcast_convert_fusion
  132.3 0.0 copy-start.5
  132.3 16.3 %while.10 = (s32[]{:T(128)}, bf16[2,32,64,256]{3,2,1,0:T(8,128)(2,1)S(1)}, f32[1024,64]{0,1:T(8,128)S(1)}, s32[2]{0:T(128)S(1)}, bf16[1024,64]{0,1:T(8,128)(2,1)...) while((s32[]{:T(128)}, ...), condition=%wide.region_3.5_spmd, body=%wide.region_2.4_spmd.sunk | while | flops 2181103616 | bytes 25297088 | solution.py:96
  132.3 0.7 dynamic_slice.15
  135.1 0.0 copy-start.2
  135.1 2.8 %add_convert_fusion.2 = (bf16[1024,32,64]{0,2,1:T(8,128)(2,1)S(1)}, bf16[1024,32,64]{0,2,1:T(8,128)(2,1)S(1)}) fusion(f32[1024,32]{0,1:T(8,128)S(1)} %get-tuple-element.129, f32[1024,64]{0,1:T(8,128)S(1)} %get-tuple-element.160, f32[1024,32]{0,1:T(8,128)S(1)} %get-tuple-element.130, f32[1024,64]{0,1:T(8,128)S(1)} %get-tuple-element.157), kind=kLoop, calls=%fused_computation.7.clone.1 | loop fusion | flops 16777216 | bytes 9175040 | tf_op jit(solution)/shard_map/while/body/eval_jaxpr/convert_element_type | solution.py:32
  137.9 0.0 copy-done.2
  137.9 2.5 bitcast_dynamic-update-slice_fusion.2
  140.5 0.7 dynamic_slice.15
  143.3 0.0 copy-start.2
  143.3 2.8 %add_convert_fusion.2 = (bf16[1024,32,64]{0,2,1:T(8,128)(2,1)S(1)}, bf16[1024,32,64]{0,2,1:T(8,128)(2,1)S(1)}) fusion(f32[1024,32]{0,1:T(8,128)S(1)} %get-tuple-element.129, f32[1024,64]{0,1:T(8,128)S(1)} %get-tuple-element.160, f32[1024,32]{0,1:T(8,128)S(1)} %get-tuple-element.130, f32[1024,64]{0,1:T(8,128)S(1)} %get-tuple-element.157), kind=kLoop, calls=%fused_computation.7.clone.1 | loop fusion | flops 16777216 | bytes 9175040 | tf_op jit(solution)/shard_map/while/body/eval_jaxpr/convert_element_type | solution.py:32
  146.1 0.0 copy-done.2
  146.1 2.5 bitcast_dynamic-update-slice_fusion.2
  148.7 0.0 copy-start.1
  148.7 1.3 copy-done.1
  150.0 0.0 reduce-scatter.2.cloned.1.call-update
  150.0 0.0 copy-done.5
  150.0 0.2 convert_reduce_fusion
  150.2 29.8 %reduce-scatter.2.cloned.1.call-done = bf16[32,64,256]{2,1,0:T(8,128)(2,1)} async-done(((bf16[64,64,256]{2,1,0:T(8,128)(2,1)}), bf16[32,64,256]{2,1,0:T(8,128)(2,1)}) %reduce-scatter.2.cloned.1.call-update) | async-done | bytes 1048592 | tf_op jit(solution)/shard_map/reduce_scatter | solution.py:97
  180.0 1.6 fusion.18
  181.6 2.3 convert_bitcast_fusion
  184.0 1.8 copy.17
  185.7 76.3 %all_to_all.18 = bf16[192,1,32,256]{3,2,1,0:T(8,128)(2,1)S(1)} all-to-all(bf16[192,1,32,256]{3,2,1,0:T(8,128)(2,1)S(1)} %copy.17), channel_id=1, replica_groups=mesh['run'=1,'row'=16,'col'=1,'seg'=2] {'row'}, dimensions={0} | all-to-all | bytes 6291456 | tf_op jit(solution)/shard_map/all_to_all | solution.py:119
  262.1 2.1 copy.18
  (15 shorter events, 0.2 us)
Async XLA Ops:
  6.5 1.0 copy-start
  6.5 118.6 %all-gather.2.cloned.1.call-start = ((), (), s32[]{:S(2)}) async-start(), calls=%async_computation.2 | async-start | bytes 4456448 | tf_op jit(solution)/shard_map/all_gather | solution.py:75
  38.8 31.9 %copy-start.4 = (s32[64]{0:T(128)S(1)}, s32[64]{0:T(128)}, u32[]{:S(2)}) copy-start(s32[64]{0:T(128)} %param.9) | copy-start | bytes 772
  70.1 2.0 copy-start.3
  72.0 108.0 %reduce-scatter.2.cloned.1.call-start = ((), (), s32[]{:S(2)}) async-start(), calls=%async_computation.3 | async-start | bytes 3145728 | tf_op jit(solution)/shard_map/reduce_scatter | solution.py:97
  132.3 17.7 %copy-start.5 = (s32[64,1]{0,1:T(1,128)S(1)}, s32[64,1]{0,1:T(1,128)}, u32[]{:S(2)}) copy-start(s32[64,1]{0,1:T(1,128)} %param.11) | copy-start | bytes 772
  135.1 2.8 %copy-start.2 = (bf16[2048,256]{1,0:T(8,128)(2,1)S(1)}, bf16[2048,256]{1,0:T(8,128)(2,1)}, u32[]{:S(2)}) copy-start(bf16[2048,256]{1,0:T(8,128)(2,1)} %get-tuple-element.162) | copy-start | bytes 3145732 | tf_op jit(solution)/shard_map/while
  143.3 2.8 %copy-start.2 = (bf16[2048,256]{1,0:T(8,128)(2,1)S(1)}, bf16[2048,256]{1,0:T(8,128)(2,1)}, u32[]{:S(2)}) copy-start(bf16[2048,256]{1,0:T(8,128)(2,1)} %get-tuple-element.162) | copy-start | bytes 3145732 | tf_op jit(solution)/shard_map/while
  148.7 1.3 copy-start.1
Sparse Core Ops, SparseCore 0:
  72.1 52.9 all-gather.1
  150.1 29.8 reduce-scatter.1
where the time goes:
time: 271 us
  blocking collectives  76.3 us (28%)
  waiting for transfers between devices  72.6 us (27%)
  matrix products  70 us (26%)
  other arithmetic  17.9 us (7%)
  local copies, waits for them, and re-layouts  16.3 us (6%)
  between operations  13.6 us (5%)
  loops' own time  4.26 us (2%)
    all_to_all x1, blocking collectives, local(): lax.all_to_all(outgoing[:, None], 'row', split_axis=0, concat_axis=1, til...  76.3 us
    all_gather x1, waiting for transfers between devices, local(): everyone = lax.all_gather(whitened, 'row', axis=1, tiled=True)  42.7 us
    dot_general x1, matrix products, local(): jnp.einsum('tf,ct->fc', sine_table, samples, preferred_element_type=jnp.f...  31.3 us
    dot_general x1, matrix products, local(): jnp.einsum('tf,ct->fc', cosine, samples, preferred_element_type=jnp.float32)  31.2 us
    reduce_scatter x1, waiting for transfers between devices, local(): lax.psum_scatter(blocks.reshape(receivers * lax.axis_size(('col', 'seg'))...  29.8 us
    convert_element_type x2, other arithmetic, correlate(): cross_real = (real_source[:, None, :] * recv_real[:, :, None] + imag_sour...  5.58 us
  transfers between devices with their start and end apart: 2, of which 2 were waited for; matrix products, arithmetic and copies ran while one was open for 4% of the time, Pallas kernels for 0%

commit v1 on v0

--- a/solution.py
+++ b/solution.py
@@ -72,7 +72,26 @@
     )
     white_real = whitened[:, :channels]
     white_imag = whitened[:, channels:]
-    everyone = lax.all_gather(whitened, "row", axis=1, tiled=True)
+    field_out = jax.lax.psum(1, axis_name="row")
+    now, wide_out, vec_out = (field_out, jax.lax.axis_index("row"), whitened.shape[1])
+    found = [(c, (c + 1) % now) for c in range(now)]
+    runs = [(c, (c - 1) % now) for c in range(now)]
+    everyone = jnp.zeros(
+        (*whitened.shape[:1], now * vec_out, *whitened.shape[1 + 1 :]), whitened.dtype
+    )
+    everyone = lax.dynamic_update_slice_in_dim(everyone, whitened, wide_out * vec_out, axis=1)
+    val = before = whitened
+    block_next = now // 2
+    for rr in range(1, block_next + 1):
+        val = jax.lax.ppermute(val, "row", found)
+        everyone = lax.dynamic_update_slice_in_dim(
+            everyone, val, (wide_out - rr) % now * vec_out, axis=1
+        )
+        if rr < now - block_next:
+            before = jax.lax.ppermute(before, axis_name="row", perm=runs)
+            everyone = lax.dynamic_update_slice_in_dim(
+                everyone, before, (wide_out + rr) % now * vec_out, axis=1
+            )
     block_ids = sources // channels
     within = sources % channels
     real_cols = block_ids * (2 * channels) + within

time: 271 us -> 293 us (1.081)
  starting transfers between devices: 0.04 us -> 30.4 us
  waiting for transfers between devices: 72.6 us -> 47.5 us
  local copies, waits for them, and re-layouts: 16.3 us -> 33.2 us
    all_gather x1 -> x0, waiting for transfers between devices: 42.7 us -> none  [local(): everyone = lax.all_gather(whitened, 'row', axis=1, tiled=True)]
    ppermute x0 -> x15, starting transfers between devices: none -> 30.4 us  [the longest x7 23.1 us: local(): before = jax.lax.ppermute(before, axis_name='row', perm=runs)]
    dynamic_update_slice x0 -> x16, local copies, waits for them, and re-layouts: none -> 15.4 us  [the longest x8 7.69 us: local(): lax.dynamic_update_slice_in_dim(everyone, val, (wide_out - rr) % now * ve...]
    ppermute x0 -> x15, waiting for transfers between devices: none -> 11.3 us  [the longest x7 6.02 us: local(): before = jax.lax.ppermute(before, axis_name='row', perm=runs)]
    reduce_scatter x1, waiting for transfers between devices: 29.8 us -> 36.1 us  [local(): lax.psum_scatter(blocks.reshape(receivers * lax.axis_size(('col', 'seg'))...]
  transfers between devices with their start and end apart: 2 -> 16, of which waited for: 2 -> 5; matrix products, arithmetic and copies ran while one was open for 4% -> 9% of each run, Pallas kernels for 0% -> 0%
where the time goes in v1:
time: 293 us; the launch traced here: 292 us
  blocking collectives  76.3 us (26%)
  matrix products  70 us (24%)
  waiting for transfers between devices  47.5 us (16%)
  local copies, waits for them, and re-layouts  33.2 us (11%)
  starting transfers between devices  30.4 us (10%)
  other arithmetic  16.9 us (6%)
  between operations  14 us (5%)
  loops' own time  4.24 us (1%)
    all_to_all x1, blocking collectives, local(): lax.all_to_all(outgoing[:, None], 'row', split_axis=0, concat_axis=1, til...  76.3 us
    reduce_scatter x1, waiting for transfers between devices, local(): lax.psum_scatter(blocks.reshape(receivers * lax.axis_size(('col', 'seg'))...  36.1 us
    dot_general x1, matrix products, local(): jnp.einsum('tf,ct->fc', sine_table, samples, preferred_element_type=jnp.f...  31.3 us
    dot_general x1, matrix products, local(): jnp.einsum('tf,ct->fc', cosine, samples, preferred_element_type=jnp.float32)  31.2 us
    ppermute x7, starting transfers between devices, local(): before = jax.lax.ppermute(before, axis_name='row', perm=runs)  23.1 us
    dynamic_update_slice x8, local copies, waits for them, and re-layouts, local(): lax.dynamic_update_slice_in_dim(everyone, val, (wide_out - rr) % now * ve...  7.69 us
    ppermute x8, starting transfers between devices, local(): val = jax.lax.ppermute(val, 'row', found)  7.32 us
    dynamic_update_slice x7, local copies, waits for them, and re-layouts, local(): lax.dynamic_update_slice_in_dim(everyone, before, (wide_out + rr) % now *...  6.95 us
  transfers between devices with their start and end apart: 16, of which 5 were waited for; matrix products, arithmetic and copies ran while one was open for 9% of the time, Pallas kernels for 0%

profile of v1, /device:TPU:1, one launch (start us, length us, event | category | flops | bytes accessed | tf_op | source)
XLA Modules:
  0.0 292.5 jit_solution(1718262741906529372)
XLA Ops:
  6.5 0.9 copy-done
  7.5 31.3 %fusion.21 = bf16[1024,64]{0,1:T(8,128)(2,1)S(1)} fusion(bf16[1,64,2048]{2,1,0:T(8,128)(2,1)S(1)} %copy-done), kind=kOutput, calls=%fused_computation.35 | convolution fusion | flops 300023808 | bytes 393216 | tf_op jit(solution)/shard_map/tf,ct->fc/dot_general | solution.py:57
  38.8 31.2 %fusion.22 = bf16[1024,64]{0,1:T(8,128)(2,1)S(1)} fusion(bf16[1,64,2048]{2,1,0:T(8,128)(2,1)S(1)} %copy-done), kind=kOutput, calls=%fused_computation.36 | convolution fusion | flops 299958272 | bytes 393216 | tf_op jit(solution)/shard_map/tf,ct->fc/dot_general | solution.py:56
  70.1 0.3 mul.197
  70.4 0.2 reduce_sum.28
  70.6 0.1 copy.15
  70.7 0.1 copy.16
  70.8 0.2 broadcast_in_dim.22
  71.0 0.2 mul.198
  71.2 0.1 multiply_convert_fusion
  71.2 2.7 collective-permute-start
  73.9 3.9 %cosine_convert_fusion.4 = bf16[1024,256]{1,0:T(8,128)(2,1)S(1)} fusion(s32[256]{0:T(256)S(1)} %iota_add_fusion), kind=kLoop, calls=%fused_computation.43 | loop fusion | flops 3932160 | bytes 525312 | tf_op jit(solution)/shard_map/convert_element_type | solution.py:23
  77.9 4.0 %fusion.31 = bf16[1024,256]{1,0:T(8,128)(2,1)S(1)} fusion(s32[256]{0:T(256)S(1)} %iota_add_fusion), kind=kLoop, calls=%fused_computation.47 | loop fusion | flops 4718592 | bytes 525312 | tf_op jit(solution)/shard_map/neg | solution.py:23
  81.9 1.0 pad_maximum_fusion
  83.0 1.8 collective-permute-start.2
  84.8 1.3 collective-permute-start.3
  86.1 2.0 collective-permute-done.2
  88.1 2.5 collective-permute-start.4
  90.6 2.5 broadcast_in_dim.21
  93.1 0.7 constant_dynamic-update-slice_fusion.15
  93.8 3.9 %collective-permute-start.5 = (bf16[1024,128]{0,1:T(8,128)(2,1)}, bf16[1024,128]{0,1:T(8,128)(2,1)}, u32[]{:S(2)}, u32[]{:S(2)}) collective-permute-start(bf16[1024,128]{0,1:T(8,128)(2,1)} %collective-permute-done.3), channel_id=1, source_target_pairs={{0,30},{2,0},{4,2},{6,4},{8,6},{10,8},{12,10},{14,12},{16,14},{18,... | collective-permute-start | bytes 786440 | tf_op jit(solution)/shard_map/ppermute | solution.py:91
  97.7 0.1 collective-permute-start.6
  98.2 0.7 constant_dynamic-update-slice_fusion.14
  98.9 3.9 %collective-permute-done.5 = bf16[1024,128]{0,1:T(8,128)(2,1)} collective-permute-done((bf16[1024,128]{0,1:T(8,128)(2,1)}, bf16[1024,128]{0,1:T(8,128)(2,1)}, u32[]{:S(2)}, u32[]{:S(2)}) %collective-permute-start.5) | collective-permute-done | bytes 262176 | tf_op jit(solution)/shard_map/ppermute | solution.py:91
  102.7 3.6 %collective-permute-start.7 = (bf16[1024,128]{0,1:T(8,128)(2,1)}, bf16[1024,128]{0,1:T(8,128)(2,1)S(1)}, u32[]{:S(2)}, u32[]{:S(2)}) collective-permute-start(bf16[1024,128]{0,1:T(8,128)(2,1)} %collective-permute-done.5), channel_id=1, source_target_pairs={{0,30},{2,0},{4,2},{6,4},{8,6},{10,8},{12,10},{14,12},{16,14},{18,... | collective-permute-start | bytes 786440 | tf_op jit(solution)/shard_map/ppermute | solution.py:91
  106.4 0.7 constant_dynamic-update-slice_fusion.13
  107.1 0.7 constant_dynamic-update-slice_fusion.12
  107.8 1.7 constant_dynamic-update-slice_fusion.11
  109.5 2.2 collective-permute-done.7
  111.6 3.6 %collective-permute-start.9 = (bf16[1024,128]{0,1:T(8,128)(2,1)S(1)}, bf16[1024,128]{0,1:T(8,128)(2,1)S(1)}, u32[]{:S(2)}, u32[]{:S(2)}) collective-permute-start(bf16[1024,128]{0,1:T(8,128)(2,1)S(1)} %collective-permute-done.7), channel_id=1, source_target_pairs={{0,30},{2,0},{4,2},{6,4},{8,6},{10,8},{12,10},{14,12},{16,14},{18,... | collective-permute-start | bytes 786440 | tf_op jit(solution)/shard_map/ppermute | solution.py:91
  115.2 1.7 constant_dynamic-update-slice_fusion.10
  116.8 1.7 constant_dynamic-update-slice_fusion.9
  118.5 1.7 constant_dynamic-update-slice_fusion.8
  120.2 4.6 %collective-permute-start.11 = (bf16[1024,128]{0,1:T(8,128)(2,1)S(1)}, bf16[1024,128]{0,1:T(8,128)(2,1)S(1)}, u32[]{:S(2)}, u32[]{:S(2)}) collective-permute-start(bf16[1024,128]{0,1:T(8,128)(2,1)S(1)} %collective-permute-done.9), channel_id=1, source_target_pairs={{0,30},{2,0},{4,2},{6,4},{8,6},{10,8},{12,10},{14,12},{16,14},{18,... | collective-permute-start | bytes 786440 | tf_op jit(solution)/shard_map/ppermute | solution.py:91
  124.8 0.7 constant_dynamic-update-slice_fusion.7
  125.5 0.7 constant_dynamic-update-slice_fusion.6
  126.3 0.7 constant_dynamic-update-slice_fusion.5
  127.0 6.1 %collective-permute-start.13 = (bf16[1024,128]{0,1:T(8,128)(2,1)S(1)}, bf16[1024,128]{0,1:T(8,128)(2,1)S(1)}, u32[]{:S(2)}, u32[]{:S(2)}) collective-permute-start(bf16[1024,128]{0,1:T(8,128)(2,1)S(1)} %collective-permute-done.11), channel_id=1, source_target_pairs={{0,30},{2,0},{4,2},{6,4},{8,6},{10,8},{12,10},{14,12},{16,14},{18,... | collective-permute-start | bytes 786440 | tf_op jit(solution)/shard_map/ppermute | solution.py:91
  133.1 0.7 constant_dynamic-update-slice_fusion.4
  133.8 0.3 collective-permute-start.14
  134.1 0.7 constant_dynamic-update-slice_fusion.3
  134.9 0.7 constant_dynamic-update-slice_fusion.2
  135.6 0.7 constant_dynamic-update-slice_fusion.1
  136.3 3.2 %collective-permute-done.14 = bf16[1024,128]{0,1:T(8,128)(2,1)S(1)} collective-permute-done((bf16[1024,128]{0,1:T(8,128)(2,1)S(1)}, bf16[1024,128]{0,1:T(8,128)(2,1)S(1)}, u32[]{:S(2)}, u32[]{:S(2)}) %collective-permute-start.14) | collective-permute-done | bytes 262176 | tf_op jit(solution)/shard_map/ppermute | solution.py:86
  139.6 0.7 constant_dynamic-update-slice_fusion
  140.3 3.5 %gather_fusion = bf16[64,1024]{1,0:T(8,128)(2,1)S(1)} fusion(bf16[1024,2048]{0,1:T(8,128)(2,1)} %constant_dynamic-update-slice_fusion, s32[1024]{0:T(1024)S(1)} %pad_clamp_fusion.1), kind=kCustom, calls=%fused_computation.clone | custom fusion | bytes 262400 | tf_op jit(solution)/shard_map/jit(_take)/gather | solution.py:98
  143.8 3.5 %gather_fusion.1 = bf16[64,1024]{1,0:T(8,128)(2,1)S(1)} fusion(bf16[1024,2048]{0,1:T(8,128)(2,1)} %constant_dynamic-update-slice_fusion, s32[1024]{0:T(1024)S(1)} %pad_clamp_fusion), kind=kCustom, calls=%fused_computation.1.clone | custom fusion | bytes 262400 | tf_op jit(solution)/shard_map/jit(_take)/gather | solution.py:99
  147.3 0.1 bitcast_convert_fusion
  147.5 16.3 %while.10 = (s32[]{:T(128)}, bf16[2,32,64,256]{3,2,1,0:T(8,128)(2,1)S(1)}, f32[1024,64]{0,1:T(8,128)S(1)}, s32[2]{0:T(128)S(1)}, bf16[1024,64]{0,1:T(8,128)(2,1)...) while((s32[]{:T(128)}, ...), condition=%wide.region_3.5_spmd, body=%wide.region_2.4_spmd.sunk | while | flops 2181103616 | bytes 25297088 | solution.py:115
  147.5 0.7 dynamic_slice.15
  150.3 2.8 add_convert_fusion.2
  153.1 2.5 bitcast_dynamic-update-slice_fusion.2
  155.6 0.7 dynamic_slice.15
  158.4 2.8 add_convert_fusion.2
  161.2 2.5 bitcast_dynamic-update-slice_fusion.2
  163.8 1.3 copy-done.1
  165.1 0.0 reduce-scatter.2.cloned.1.call-update
  165.1 0.2 convert_reduce_fusion
  165.3 36.1 %reduce-scatter.2.cloned.1.call-done = bf16[32,64,256]{2,1,0:T(8,128)(2,1)} async-done(((bf16[64,64,256]{2,1,0:T(8,128)(2,1)}), bf16[32,64,256]{2,1,0:T(8,128)(2,1)}) %reduce-scatter.2.cloned.1.call-update) | async-done | bytes 1048592 | tf_op jit(solution)/shard_map/reduce_scatter | solution.py:116
  201.5 1.6 fusion.18
  203.1 2.3 convert_bitcast_fusion
  205.4 1.8 copy.17
  207.2 76.3 %all_to_all.18 = bf16[192,1,32,256]{3,2,1,0:T(8,128)(2,1)S(1)} all-to-all(bf16[192,1,32,256]{3,2,1,0:T(8,128)(2,1)S(1)} %copy.17), channel_id=1, replica_groups=mesh['run'=1,'row'=16,'col'=1,'seg'=2] {'row'}, dimensions={0} | all-to-all | bytes 6291456 | tf_op jit(solution)/shard_map/all_to_all | solution.py:138
  283.5 2.1 copy.18
  (44 shorter events, 0.3 us)
Async XLA Ops:
  6.5 1.0 copy-start
  6.5 194.9 %reduce-scatter.2.cloned.1.call-start = ((), (), s32[]{:S(2)}) async-start(), calls=%async_computation.2 | async-start | bytes 3145728 | tf_op jit(solution)/shard_map/reduce_scatter | solution.py:116
  38.8 31.9 %copy-start.4 = (s32[64]{0:T(128)S(1)}, s32[64]{0:T(128)}, u32[]{:S(2)}) copy-start(s32[64]{0:T(128)} %param.9) | copy-start | bytes 772
  70.1 12.8 %copy-start.3 = (s32[64]{0:T(128)S(1)}, s32[64]{0:T(128)}, u32[]{:S(2)}) copy-start(s32[64]{0:T(128)} %param.10) | copy-start | bytes 772
  71.2 11.8 %collective-permute-start = (bf16[1024,128]{0,1:T(8,128)(2,1)S(1)}, bf16[1024,128]{0,1:T(8,128)(2,1)S(1)}, u32[]{:S(2)}, u32[]{:S(2)}) collective-permute-start(bf16[1024,128]{0,1:T(8,128)(2,1)S(1)} %bitcast.42), channel_id=1, source_target_pairs={{0,2},{2,4},{4,6},{6,8},{8,10},{10,12},{12,14},{14,16},{16,18},{18... | collective-permute-start | bytes 786440 | tf_op jit(solution)/shard_map/ppermute | solution.py:86
  73.9 10.9 %collective-permute-start.1 = (bf16[1024,128]{0,1:T(8,128)(2,1)S(1)}, bf16[1024,128]{0,1:T(8,128)(2,1)S(1)}, u32[]{:S(2)}, u32[]{:S(2)}) collective-permute-start(bf16[1024,128]{0,1:T(8,128)(2,1)S(1)} %bitcast.43), channel_id=1, source_target_pairs={{0,30},{2,0},{4,2},{6,4},{8,6},{10,8},{12,10},{14,12},{16,14},{18,... | collective-permute-start | bytes 786440 | tf_op jit(solution)/shard_map/ppermute | solution.py:91
  83.0 5.1 %collective-permute-start.2 = (bf16[1024,128]{0,1:T(8,128)(2,1)S(1)}, bf16[1024,128]{0,1:T(8,128)(2,1)S(1)}, u32[]{:S(2)}, u32[]{:S(2)}) collective-permute-start(bf16[1024,128]{0,1:T(8,128)(2,1)S(1)} %collective-permute-done), channel_id=1, source_target_pairs={{0,2},{2,4},{4,6},{6,8},{8,10},{10,12},{12,14},{14,16},{16,18},{18... | collective-permute-start | bytes 786440 | tf_op jit(solution)/shard_map/ppermute | solution.py:86
  84.8 9.0 %collective-permute-start.3 = (bf16[1024,128]{0,1:T(8,128)(2,1)S(1)}, bf16[1024,128]{0,1:T(8,128)(2,1)}, u32[]{:S(2)}, u32[]{:S(2)}) collective-permute-start(bf16[1024,128]{0,1:T(8,128)(2,1)S(1)} %collective-permute-done.1), channel_id=1, source_target_pairs={{0,30},{2,0},{4,2},{6,4},{8,6},{10,8},{12,10},{14,12},{16,14},{18,... | collective-permute-start | bytes 786440 | tf_op jit(solution)/shard_map/ppermute | solution.py:91
  88.1 9.6 %collective-permute-start.4 = (bf16[1024,128]{0,1:T(8,128)(2,1)S(1)}, bf16[1024,128]{0,1:T(8,128)(2,1)}, u32[]{:S(2)}, u32[]{:S(2)}) collective-permute-start(bf16[1024,128]{0,1:T(8,128)(2,1)S(1)} %collective-permute-done.2), channel_id=1, source_target_pairs={{0,2},{2,4},{4,6},{6,8},{8,10},{10,12},{12,14},{14,16},{16,18},{18... | collective-permute-start | bytes 786440 | tf_op jit(solution)/shard_map/ppermute | solution.py:86
  93.8 8.9 %collective-permute-start.5 = (bf16[1024,128]{0,1:T(8,128)(2,1)}, bf16[1024,128]{0,1:T(8,128)(2,1)}, u32[]{:S(2)}, u32[]{:S(2)}) collective-permute-start(bf16[1024,128]{0,1:T(8,128)(2,1)} %collective-permute-done.3), channel_id=1, source_target_pairs={{0,30},{2,0},{4,2},{6,4},{8,6},{10,8},{12,10},{14,12},{16,14},{18,... | collective-permute-start | bytes 786440 | tf_op jit(solution)/shard_map/ppermute | solution.py:91
  97.7 9.3 %collective-permute-start.6 = (bf16[1024,128]{0,1:T(8,128)(2,1)}, bf16[1024,128]{0,1:T(8,128)(2,1)}, u32[]{:S(2)}, u32[]{:S(2)}) collective-permute-start(bf16[1024,128]{0,1:T(8,128)(2,1)} %collective-permute-done.4), channel_id=1, source_target_pairs={{0,2},{2,4},{4,6},{6,8},{8,10},{10,12},{12,14},{14,16},{16,18},{18... | collective-permute-start | bytes 786440 | tf_op jit(solution)/shard_map/ppermute | solution.py:86
  102.7 8.9 %collective-permute-start.7 = (bf16[1024,128]{0,1:T(8,128)(2,1)}, bf16[1024,128]{0,1:T(8,128)(2,1)S(1)}, u32[]{:S(2)}, u32[]{:S(2)}) collective-permute-start(bf16[1024,128]{0,1:T(8,128)(2,1)} %collective-permute-done.5), channel_id=1, source_target_pairs={{0,30},{2,0},{4,2},{6,4},{8,6},{10,8},{12,10},{14,12},{16,14},{18,... | collective-permute-start | bytes 786440 | tf_op jit(solution)/shard_map/ppermute | solution.py:91
  107.1 9.8 %collective-permute-start.8 = (bf16[1024,128]{0,1:T(8,128)(2,1)}, bf16[1024,128]{0,1:T(8,128)(2,1)S(1)}, u32[]{:S(2)}, u32[]{:S(2)}) collective-permute-start(bf16[1024,128]{0,1:T(8,128)(2,1)} %collective-permute-done.6), channel_id=1, source_target_pairs={{0,2},{2,4},{4,6},{6,8},{8,10},{10,12},{12,14},{14,16},{16,18},{18... | collective-permute-start | bytes 786440 | tf_op jit(solution)/shard_map/ppermute | solution.py:86
  111.6 8.6 %collective-permute-start.9 = (bf16[1024,128]{0,1:T(8,128)(2,1)S(1)}, bf16[1024,128]{0,1:T(8,128)(2,1)S(1)}, u32[]{:S(2)}, u32[]{:S(2)}) collective-permute-start(bf16[1024,128]{0,1:T(8,128)(2,1)S(1)} %collective-permute-done.7), channel_id=1, source_target_pairs={{0,30},{2,0},{4,2},{6,4},{8,6},{10,8},{12,10},{14,12},{16,14},{18,... | collective-permute-start | bytes 786440 | tf_op jit(solution)/shard_map/ppermute | solution.py:91
  116.8 8.7 %collective-permute-start.10 = (bf16[1024,128]{0,1:T(8,128)(2,1)S(1)}, bf16[1024,128]{0,1:T(8,128)(2,1)S(1)}, u32[]{:S(2)}, u32[]{:S(2)}) collective-permute-start(bf16[1024,128]{0,1:T(8,128)(2,1)S(1)} %collective-permute-done.8), channel_id=1, source_target_pairs={{0,2},{2,4},{4,6},{6,8},{8,10},{10,12},{12,14},{14,16},{16,18},{18... | collective-permute-start | bytes 786440 | tf_op jit(solution)/shard_map/ppermute | solution.py:86
  120.2 6.8 %collective-permute-start.11 = (bf16[1024,128]{0,1:T(8,128)(2,1)S(1)}, bf16[1024,128]{0,1:T(8,128)(2,1)S(1)}, u32[]{:S(2)}, u32[]{:S(2)}) collective-permute-start(bf16[1024,128]{0,1:T(8,128)(2,1)S(1)} %collective-permute-done.9), channel_id=1, source_target_pairs={{0,30},{2,0},{4,2},{6,4},{8,6},{10,8},{12,10},{14,12},{16,14},{18,... | collective-permute-start | bytes 786440 | tf_op jit(solution)/shard_map/ppermute | solution.py:91
  125.5 8.3 %collective-permute-start.12 = (bf16[1024,128]{0,1:T(8,128)(2,1)S(1)}, bf16[1024,128]{0,1:T(8,128)(2,1)S(1)}, u32[]{:S(2)}, u32[]{:S(2)}) collective-permute-start(bf16[1024,128]{0,1:T(8,128)(2,1)S(1)} %collective-permute-done.10), channel_id=1, source_target_pairs={{0,2},{2,4},{4,6},{6,8},{8,10},{10,12},{12,14},{14,16},{16,18},{18... | collective-permute-start | bytes 786440 | tf_op jit(solution)/shard_map/ppermute | solution.py:86
  127.0 8.6 %collective-permute-start.13 = (bf16[1024,128]{0,1:T(8,128)(2,1)S(1)}, bf16[1024,128]{0,1:T(8,128)(2,1)S(1)}, u32[]{:S(2)}, u32[]{:S(2)}) collective-permute-start(bf16[1024,128]{0,1:T(8,128)(2,1)S(1)} %collective-permute-done.11), channel_id=1, source_target_pairs={{0,30},{2,0},{4,2},{6,4},{8,6},{10,8},{12,10},{14,12},{16,14},{18,... | collective-permute-start | bytes 786440 | tf_op jit(solution)/shard_map/ppermute | solution.py:91
  133.8 5.7 %collective-permute-start.14 = (bf16[1024,128]{0,1:T(8,128)(2,1)S(1)}, bf16[1024,128]{0,1:T(8,128)(2,1)S(1)}, u32[]{:S(2)}, u32[]{:S(2)}) collective-permute-start(bf16[1024,128]{0,1:T(8,128)(2,1)S(1)} %collective-permute-done.12), channel_id=1, source_target_pairs={{0,2},{2,4},{4,6},{6,8},{8,10},{10,12},{12,14},{14,16},{16,18},{18... | collective-permute-start | bytes 786440 | tf_op jit(solution)/shard_map/ppermute | solution.py:86
  147.5 17.7 %copy-start.5 = (s32[64,1]{0,1:T(1,128)S(1)}, s32[64,1]{0,1:T(1,128)}, u32[]{:S(2)}) copy-start(s32[64,1]{0,1:T(1,128)} %param.11) | copy-start | bytes 772
  150.3 2.8 copy-start.2
  158.4 2.8 copy-start.2
  163.8 1.3 copy-start.1
Sparse Core Ops, SparseCore 0:
  165.3 36.1 reduce-scatter.1
